TPU v7x, 256 devices: a whole 4x4x8 slice. The times are simulated.
256 devices in a mesh: energy: 64 (over z, x, core), mom: 4 (over y).
Axes of the slice: x: 4, y: 4, z: 8, core: 2. Of those that a mesh axis runs over, the one named last changes fastest.
Arguments:
- green_less: float32 [4, 64, 64, 64, 128], P('mom', 'energy'), may hold values from -6 to 6
- couplings: bfloat16 [32, 3, 64, 64], replicated, may hold values from -0.75 to 0.75
- pair_atoms: int32 [64, 2], replicated, may hold values from 0 to 31
- shift_idx: int32 [3], replicated, may hold values from 1 to 4, as said below
- weights: float32 [2, 3, 4], replicated, may hold values from 0.05 to 1
Outputs:
- sigma_less: float32 [4, 64, 64, 64, 128], P('mom', 'energy')
Inputs may be any that keep to these rules, and one draw needn't show every extreme that they name: `shift_idx`: one mode's shift is exactly 4 and another's is exactly 1.
All inputs are finite; a program needn't handle non-finite values.
Results may differ from a plain program's by a relative error of at most 0.0003.
Values sent between devices are 32-bit elements; how exact they have to be, the bound alone decides.
No kernel may reach another device: no remote copies, remote signals or barrier semaphores. Data moves between devices by JAX's collectives and lax.ppermute only.
A program may use at most 64 MiB of HBM per device.

v0:
```python
import functools
import itertools

import jax
import jax.numpy as jnp
from jax import lax
from jax.experimental import pallas as pl
from jax.experimental.pallas import tpu as pltpu
from jax.sharding import Mesh
from jax.sharding import PartitionSpec as P

NMODE = 3
VMEM_BYTES = 16 * 2**20
LIMIT = pltpu.CompilerParams(vmem_limit_bytes=VMEM_BYTES)
GROUP = ("x", "c", "y")
AXES = ("z", "x", "c", "y")


def tables_kernel(atoms, coupling_hbm, left_ref, right_ref, picked, sems):
    pairs = left_ref.shape[0]
    copies = []
    for pair in range(pairs):
        for side in range(2):
            copy = pltpu.make_async_copy(
                coupling_hbm.at[atoms[pair, side]], picked.at[pair, side], sems.at[pair, side]
            )
            copy.start()
            copies.append(copy)
    for copy in copies:
        copy.wait()
    size = picked.shape[-1]
    nothing = jnp.zeros((size, size), jnp.float32)
    for pair in range(pairs):
        lefts = []
        for mode in range(NMODE):
            left = picked[pair, 0, mode].astype(jnp.float32)
            lefts += [left, left]
            turned = picked[pair, 1, mode].astype(jnp.float32).T
            upper = jnp.concatenate([turned, nothing], axis=1)
            lower = jnp.concatenate([nothing, turned], axis=1)
            both = jnp.concatenate([upper, lower], axis=0).astype(jnp.bfloat16)
            right_ref[pair, mode, 0] = both
            right_ref[pair, mode, 1] = both
        left_ref[pair] = jnp.concatenate(lefts, axis=1).astype(jnp.bfloat16)


def tables(atoms, couplings):
    pairs, size = atoms.shape[0], couplings.shape[-1]
    return pl.pallas_call(
        tables_kernel,
        grid_spec=pltpu.PrefetchScalarGridSpec(
            num_scalar_prefetch=1,
            grid=(1,),
            in_specs=[pl.BlockSpec(memory_space=pl.ANY)],
            out_specs=[
                pl.BlockSpec((pairs, size, 2 * NMODE * size), lambda i, a: (0, 0, 0)),
                pl.BlockSpec((pairs, NMODE, 2, 2 * size, 2 * size), lambda i, a: (0, 0, 0, 0, 0)),
            ],
            scratch_shapes=[
                pltpu.VMEM((pairs, 2, NMODE, size, size), jnp.bfloat16),
                pltpu.SemaphoreType.DMA((pairs, 2)),
            ],
        ),
        out_shape=[
            jax.ShapeDtypeStruct((pairs, size, 2 * NMODE * size), jnp.bfloat16),
            jax.ShapeDtypeStruct((pairs, NMODE, 2, 2 * size, 2 * size), jnp.bfloat16),
        ],
        compiler_params=LIMIT,
        cost_estimate=pl.CostEstimate(flops=1000000, bytes_accessed=4000000, transcendentals=0),
        name="tables",
    )(atoms, couplings)


def fold_kernel(block_ref, low_ref, high_ref):
    half = low_ref.shape[0]
    for energy in range(2 * half):
        target = low_ref if energy < half else high_ref
        first, second, third, fourth = (block_ref[energy, moment] for moment in range(4))
        even, odd = first + third, second + fourth
        target[energy % half, 0] = even + odd
        target[energy % half, 1] = even - odd
        target[energy % half, 2] = first - third
        target[energy % half, 3] = second - fourth


def fold(block, pair):
    energies, moments, _, rows, columns = block.shape
    half = (energies // 2, moments, rows, columns)
    vmem = pl.BlockSpec(half, lambda i: (0, 0, 0, 0))
    return pl.pallas_call(
        fold_kernel,
        grid=(1,),
        in_specs=[
            pl.BlockSpec((energies, moments, None, rows, columns), lambda i: (0, 0, pair, 0, 0))
        ],
        out_specs=[vmem, vmem],
        out_shape=[jax.ShapeDtypeStruct(half, jnp.float32)] * 2,
        compiler_params=LIMIT,
        cost_estimate=pl.CostEstimate(flops=1000000, bytes_accessed=4000000, transcendentals=0),
        name="fold",
    )(block)


def mix_kernel(split, pair, place, shifts, weights, left_ref, right_ref, *rest):
    if split:
        *quarters, kept_ref, away_ref, window, out_ref = rest
    else:
        *quarters, result, window, out_ref, sems = rest
    quarter = quarters[0].shape[0]
    targets = quarter * (len(quarters) - 2)
    for spot, part in enumerate(quarters):
        for energy in range(quarter):
            window[spot * quarter + energy] = part[energy]
    factors = []
    for mode in range(NMODE):
        for side in range(2):
            w0, w1, w2, w3 = (weights[side, mode, moment] for moment in range(4))
            even, odd = w0 + w2, w1 + w3
            factors.append(
                ((even + odd) * 0.25, (even - odd) * 0.25, (w0 - w2) * 0.5, (w1 - w3) * 0.5)
            )
    rows = window.shape[2]

    def one_energy(energy, carry):
        stacked = [[] for _ in range(4)]
        for mode in range(NMODE):
            shift = shifts[mode]
            parts = []
            for side, spot in ((0, energy + quarter - shift), (1, energy + quarter + shift)):
                p, q, r, s = factors[2 * mode + side]
                total, swing, d0, d1 = (window[spot, part] for part in range(4))
                parts.append((p * total, q * swing, r * d0 - s * d1, s * d0 + r * d1))
            mixed = jnp.concatenate([a + b for a, b in zip(*parts)], axis=0)
            coarse = mixed.astype(jnp.bfloat16)
            fine = (mixed - coarse.astype(jnp.float32)).astype(jnp.bfloat16)
            right = right_ref[pair, mode].reshape(2 * right_ref.shape[3], right_ref.shape[4])
            product = jnp.dot(
                jnp.concatenate([coarse, fine], axis=1), right, preferred_element_type=jnp.float32
            )
            coarse = product.astype(jnp.bfloat16)
            fine = (product - coarse.astype(jnp.float32)).astype(jnp.bfloat16)
            for part in range(4):
                block = slice(part * rows, (part + 1) * rows)
                stacked[part] += [coarse[block], fine[block]]
        columns = jnp.concatenate([jnp.concatenate(pieces, axis=0) for pieces in stacked], axis=1)
        total = jnp.dot(left_ref[pair], columns, preferred_element_type=jnp.float32)
        width = out_ref.shape[-1]
        plain, swing, v0, v1 = (total[:, part * width : (part + 1) * width] for part in range(4))
        even, odd = plain + swing, plain - swing
        for moment, value in enumerate((even + v0, odd + v1, even - v0, odd - v1)):
            if split:
                away = jnp.where(lax.rem(energy, 2) == place[0], 0, 1)
                out_ref[away, energy // 2, moment] = value
            else:
                out_ref[energy, moment] = value
        if not split:
            pltpu.make_async_copy(out_ref.at[energy], result.at[energy], sems.at[energy]).start()
        return carry

    lax.fori_loop(0, targets, one_energy, 0, unroll=targets)
    if not split:
        for energy in range(targets):
            pltpu.make_async_copy(out_ref.at[energy], result.at[energy], sems.at[energy]).wait()
    if split:
        for x in range(kept_ref.shape[0]):
            kept_ref[x] = out_ref[0, x]
            away_ref[x] = out_ref[1, x]


def mix(split, place, shifts, weights, quarters, left, right, pair):
    quarter, moments, rows, columns = quarters[0].shape
    targets = quarter * (len(quarters) - 2)
    vmem = pl.BlockSpec(memory_space=pltpu.VMEM)
    smem = pl.BlockSpec(memory_space=pltpu.SMEM)
    scratch = [pltpu.VMEM((quarter * len(quarters), moments, rows, columns), jnp.float32)]
    if split:
        shape, outs = (targets // 2, moments, rows, columns), [vmem, vmem]
        scratch += [pltpu.VMEM((2, *shape), jnp.float32)]
    else:
        shape, outs = (targets, moments, rows, columns), [pl.BlockSpec(memory_space=pl.ANY)]
        scratch += [pltpu.VMEM(shape, jnp.float32), pltpu.SemaphoreType.DMA((targets,))]
    return pl.pallas_call(
        functools.partial(mix_kernel, split, pair),
        in_specs=[smem] * 3 + [vmem] * (2 + len(quarters)),
        out_specs=outs,
        out_shape=[jax.ShapeDtypeStruct(shape, jnp.float32) for _ in outs],
        scratch_shapes=scratch,
        compiler_params=LIMIT,
        cost_estimate=pl.CostEstimate(flops=2500000000, bytes_accessed=2000000, transcendentals=0),
        name="mix",
    )(place, shifts, weights, left, right, *quarters)


def sort_kernel(place, kept_low, kept_high, received_low, received_high, *targets):
    core, first = place[0], place[1]
    half = kept_low.shape[0]
    whole = targets[-1]
    targets = targets[:-1]
    for side, pieces in enumerate(((kept_low, kept_high), (received_low, received_high))):
        for x in range(2 * half):
            whole[side, x] = pieces[x // half][x % half]
    for step, target in enumerate(targets):
        where = lax.rem(first + step, 4)
        for other in range(4):
            x = jnp.where(core == 0, other, where)
            moment = jnp.where(core == 0, where, other)
            target[core, other] = whole[0, x, moment]
            target[1 - core, other] = whole[1, x, moment]


def turn_kernel(place, *refs):
    sources, targets = refs[:4], refs[4:]
    for step, target in enumerate(targets):
        column = lax.rem(place[2] + step, 4)
        for behind, source in enumerate(sources):
            for owner in range(2):
                target[behind, owner] = source[owner, column]


def move(kernel, place, arrays, shape, scratch=()):
    vmem = pl.BlockSpec(memory_space=pltpu.VMEM)
    return list(
        pl.pallas_call(
            kernel,
            in_specs=[pl.BlockSpec(memory_space=pltpu.SMEM)] + [vmem] * len(arrays),
            out_specs=[vmem] * 4,
            out_shape=[jax.ShapeDtypeStruct(shape, jnp.float32)] * 4,
            scratch_shapes=scratch,
            compiler_params=LIMIT,
            cost_estimate=pl.CostEstimate(flops=1000000, bytes_accessed=2000000, transcendentals=0),
        )(place, *arrays)
    )


def place_kernel(place, held, *rest):
    sources, (out, sems) = rest[:4], rest[4:]
    core, first, second = place[0], place[1], place[2]
    copies = []
    for step, source in enumerate(sources):
        along_second = lax.rem(second + 4 - step, 4)
        for behind in range(4):
            along_first = lax.rem(first + 4 - behind, 4)
            x = jnp.where(core == 0, along_second, along_first)
            y = jnp.where(core == 0, along_first, along_second)
            copies.append(
                pltpu.make_async_copy(
                    source.at[behind], out.at[x, :, y, 0], sems.at[step, behind]
                )
            )
    for copy in copies:
        copy.start()
    for copy in copies:
        copy.wait()


def fill_kernel(back, out, sem):
    copy = pltpu.make_async_copy(back, out.at[:, :, :, 1], sem.at[0])
    copy.start()
    copy.wait()


def put(place, landed, back):
    rows, columns = back.shape[1:]
    hbm = pl.BlockSpec(memory_space=pl.ANY)
    result = jax.ShapeDtypeStruct((4, 2, 4, 2, rows, columns), jnp.float32)
    cost = pl.CostEstimate(flops=1000000, bytes_accessed=4000000, transcendentals=0)
    half = pl.pallas_call(
        fill_kernel,
        in_specs=[hbm],
        out_specs=hbm,
        out_shape=result,
        scratch_shapes=[pltpu.SemaphoreType.DMA((1,))],
        compiler_params=LIMIT,
        cost_estimate=cost,
        name="fill",
    )(back.reshape(4, 2, 4, rows, columns))
    return pl.pallas_call(
        place_kernel,
        in_specs=[pl.BlockSpec(memory_space=pltpu.SMEM)] + [hbm] * 5,
        out_specs=hbm,
        out_shape=result,
        scratch_shapes=[pltpu.SemaphoreType.DMA((4, 4))],
        input_output_aliases={1: 0},
        compiler_params=LIMIT,
        cost_estimate=cost,
        name="place",
    )(place, half, *landed)


def ring(fn):
    sizes = [lax.axis_size(axis) for axis in AXES]
    pairs = []
    for z, x, c, y in itertools.product(*map(range, sizes)):
        tx, tc, ty = fn(x, c, y)
        pairs.append((((z * sizes[1] + x) * sizes[2] + c) * sizes[3] + y,
                      ((z * sizes[1] + tx % 4) * sizes[2] + tc) * sizes[3] + ty % 4))
    return pairs


def along(step, core):
    return ring(lambda x, c, y: (x, c, y + step) if c == core else (x + step, c, y))


def on_device(green_less, couplings, pair_atoms, shift_idx, weights):
    pairs, rows, columns = green_less.shape[2:]
    group = lax.axis_size(GROUP)
    moments = lax.axis_size("y")
    planes = lax.axis_size("z")
    here = lax.axis_index(GROUP)
    up = [(plane, plane + 1) for plane in range(planes - 1)]
    down = [(plane + 1, plane) for plane in range(planes - 1)]
    owned = pairs // group
    atoms = lax.dynamic_slice_in_dim(pair_atoms, here * owned, owned, 0)
    couplings = pltpu.with_memory_space_constraint(couplings, pltpu.HBM)
    x, c, y = (lax.axis_index(axis) for axis in GROUP)
    first, second = jnp.where(c == 0, y, x), jnp.where(c == 0, x, y)
    place = jnp.stack([c, first, second]).astype(jnp.int32)
    left, right = tables(atoms, couplings)
    moved = lax.all_to_all(
        green_less.reshape(group, owned, rows, columns), GROUP, 0, 0, tiled=True
    )
    block = moved.reshape(group // moments, moments, owned, rows, columns)
    halves = []
    for pair in range(owned):
        low, high = fold(block, pair)
        below = lax.ppermute(high, "z", up)
        above = lax.ppermute(low, "z", down)
        halves.append((below, low, high, above))

    def compute(split, pair, first_quarter, count):
        quarters = halves[pair][first_quarter : first_quarter + count]
        return mix(split, place, shift_idx, weights, quarters, left, right, pair)

    kept, received = [], []
    for upper in range(2):
        stay, away = compute(True, 0, upper, 3)
        received.append(lax.ppermute(away, AXES, ring(lambda x, c, y: (x, 1 - c, y))))
        kept.append(stay)
    arrived = move(
        sort_kernel,
        place,
        (*kept, *received),
        (2, 4, rows, columns),
        [pltpu.VMEM((2, 4, 4, rows, columns), jnp.float32)],
    )
    for step in (2, 1, 3):
        arrived[step] = lax.ppermute(arrived[step], AXES, along(step, 0))
    (result,) = compute(False, 1, 0, 4)
    back = lax.all_to_all(result.reshape(group, rows, columns), GROUP, 0, 0, tiled=True)
    landed = move(turn_kernel, place, arrived, (4, 2, rows, columns))
    for step in (2, 1, 3):
        landed[step] = lax.ppermute(landed[step], AXES, along(step, 1))
    return put(place, landed, back).reshape(green_less.shape)


def solution(mesh):
    sizes = dict(mesh.shape)
    chips = sizes["energy"] // 8
    split = Mesh(
        mesh.devices.reshape(chips, 4, 2, sizes["mom"]), ("z", "x", "c", "y")
    )
    placed = P("y", ("z", "x", "c"), None, None, None)

    return jax.shard_map(
        on_device,
        mesh=split,
        in_specs=(placed, P(), P(), P(), P()),
        out_specs=placed,
        check_vma=False,
    )
```

profile of v0, /device:TPU:96, one launch (start us, length us, event | category | flops | bytes accessed | tf_op | source)
XLA Modules:
  0.0 102.7 jit_solution(11629884532707407805)
XLA Ops:
  0.0 0.0 copy-start
  0.0 35.7 %all_to_all.10 = f32[32,2,64,128]{3,2,1,0:T(8,128)S(1)} all-to-all(f32[32,2,64,128]{3,2,1,0:T(8,128)} %bitcast.11), channel_id=1, replica_groups=mesh['z'=8,'x'=4,'c'=2,'y'=4] {'x','c','y'}, dimensions={0} | all-to-all | bytes 4194304 | tf_op jit(solution)/shard_map/all_to_all | solution.py:319
  35.7 0.0 copy-start.2
  35.7 0.1 fold.2
  35.8 0.0 copy-start.1
  35.8 5.0 %collective-permute-start = (f32[4,4,64,128]{3,2,1,0:T(8,128)S(1)}, f32[4,4,64,128]{3,2,1,0:T(8,128)S(1)}, u32[]{:S(2)}, u32[]{:S(2)}) collective-permute-start(f32[4,4,64,128]{3,2,1,0:T(8,128)S(1)} %get-tuple-element.25.rest_2_), channel_id=1, source_target_pairs={{0,32},{32,64},{64,96},{96,128},{128,160},{160,192},{192,224},{1,3... | collective-permute-start | bytes 1572872 | tf_op jit(solution)/shard_map/ppermute | solution.py:326
  40.9 1.9 %collective-permute-start.1 = (f32[4,4,64,128]{3,2,1,0:T(8,128)S(1)}, f32[4,4,64,128]{3,2,1,0:T(8,128)}, u32[]{:S(2)}, u32[]{:S(2)}) collective-permute-start(f32[4,4,64,128]{3,2,1,0:T(8,128)S(1)} %get-tuple-element.26.rest_1_), channel_id=1, source_target_pairs={{32,0},{64,32},{96,64},{128,96},{160,128},{192,160},{224,192},{33,... | collective-permute-start | bytes 1572872 | tf_op jit(solution)/shard_map/ppermute | solution.py:327
  42.8 0.1 fold.3
  42.9 5.1 %collective-permute-start.2 = (f32[4,4,64,128]{3,2,1,0:T(8,128)S(1)}, f32[4,4,64,128]{3,2,1,0:T(8,128)}, u32[]{:S(2)}, u32[]{:S(2)}) collective-permute-start(f32[4,4,64,128]{3,2,1,0:T(8,128)S(1)} %get-tuple-element.27.rest_2_.rest_1_), channel_id=1, source_target_pairs={{0,32},{32,64},{64,96},{96,128},{128,160},{160,192},{192,224},{1,3... | collective-permute-start | bytes 1572872 | tf_op jit(solution)/shard_map/ppermute | solution.py:326
  48.0 0.0 copy-done
  48.1 0.1 constant_dynamic-slice_fusion
  48.1 1.9 %collective-permute-start.3 = (f32[4,4,64,128]{3,2,1,0:T(8,128)S(1)}, f32[4,4,64,128]{3,2,1,0:T(8,128)}, u32[]{:S(2)}, u32[]{:S(2)}) collective-permute-start(f32[4,4,64,128]{3,2,1,0:T(8,128)S(1)} %get-tuple-element.28.rest_1_.rest_0_), channel_id=1, source_target_pairs={{32,0},{64,32},{96,64},{128,96},{160,128},{192,160},{224,192},{33,... | collective-permute-start | bytes 1572872 | tf_op jit(solution)/shard_map/ppermute | solution.py:327
  50.0 0.1 pad_add_fusion.place
  50.1 0.1 copy.11.atoms
  50.2 0.0 copy-done.2
  50.2 1.7 %tables.1 = (bf16[2,64,384]{2,1,0:T(8,128)(2,1)S(1)}, bf16[2,3,2,128,128]{4,3,2,1,0:T(8,128)(2,1)S(1)}) custom-call(s32[2,2]{1,0:T(2,128)S(1)} %copy.11.atoms, bf16[32,3,64,64]{3,2,1,0:T(8,128)(2,1)} %coupling_hbm.1), custom_call_target="tpu_custom_call" | custom-call | flops 1000000 | bytes 4000000 | tf_op jit(solution)/shard_map/tables/pallas_call | solution.py:49
  51.9 1.2 %collective-permute-done.rest_0_ = f32[4,4,64,128]{3,2,1,0:T(8,128)S(1)} collective-permute-done((f32[4,4,64,128]{3,2,1,0:T(8,128)S(1)}, f32[4,4,64,128]{3,2,1,0:T(8,128)S(1)}, u32[]{:S(2)}, u32[]{:S(2)}) %collective-permute-start) | collective-permute-done | bytes 524320 | tf_op jit(solution)/shard_map/ppermute | solution.py:326
  53.2 5.7 %collective-permute-done.1.rest_3_ = f32[4,4,64,128]{3,2,1,0:T(8,128)} collective-permute-done((f32[4,4,64,128]{3,2,1,0:T(8,128)S(1)}, f32[4,4,64,128]{3,2,1,0:T(8,128)}, u32[]{:S(2)}, u32[]{:S(2)}) %collective-permute-start.1) | collective-permute-done | bytes 524320 | tf_op jit(solution)/shard_map/ppermute | solution.py:327
  58.9 0.0 copy-done.1
  58.9 4.2 %mix.3 = f32[8,4,64,128]{3,2,1,0:T(8,128)} custom-call(s32[3]{0:T(128)S(1)} %pad_add_fusion.place, s32[3]{0:T(128)S(1)} %copy-done.1, f32[2,3,4]{2,1,0:T(4,128)S(1)} %copy.8.weights, bf16[2,64,384]{2,1,0:T(8,128)(2,1)S(1)} %get-tuple-element.23.left_ref, bf16[2,3,2,128,128]{4,3,2,1,0:T(8,128)(2,1)S(1)} %get-tuple-element.24.right_ref, ...), custom_call_target="tpu_custom_call" | custom-call | flops 2500000000 | bytes 2000000 | tf_op jit(solution)/shard_map/mix/pallas_call | solution.py:182
  63.1 3.9 %all-to-all-start.1 = ((f32[32,64,128]{2,1,0:T(8,128)}), f32[32,64,128]{2,1,0:T(8,128)S(1)}, u32[]{:S(2)}, u32[]{:S(2)}) async-start(f32[32,64,128]{2,1,0:T(8,128)} %bitcast.5), calls=%async_computation.1 | async-start | bytes 2097152 | tf_op jit(solution)/shard_map/all_to_all | solution.py:349
  67.0 0.0 collective-permute-done.2.rest_0_
  67.1 2.4 %mix.4 = (f32[2,4,64,128]{3,2,1,0:T(8,128)S(1)}, f32[2,4,64,128]{3,2,1,0:T(8,128)S(1)}) custom-call(s32[3]{0:T(128)S(1)} %pad_add_fusion.place, s32[3]{0:T(128)S(1)} %copy-done.1, f32[2,3,4]{2,1,0:T(4,128)S(1)} %copy.8.weights, bf16[2,64,384]{2,1,0:T(8,128)(2,1)S(1)} %get-tuple-element.23.left_ref, ...), custom_call_target="tpu_custom_call" | custom-call | flops 2500000000 | bytes 2000000 | tf_op jit(solution)/shard_map/mix/pallas_call | solution.py:182
  69.5 0.3 collective-permute-start.4
  69.8 0.0 collective-permute-done.3.rest_2_
  69.8 2.4 %mix.5 = (f32[2,4,64,128]{3,2,1,0:T(8,128)S(1)}, f32[2,4,64,128]{3,2,1,0:T(8,128)S(1)}) custom-call(s32[3]{0:T(128)S(1)} %pad_add_fusion.place, s32[3]{0:T(128)S(1)} %copy-done.1, f32[2,3,4]{2,1,0:T(4,128)S(1)} %copy.8.weights, bf16[2,64,384]{2,1,0:T(8,128)(2,1)S(1)} %get-tuple-element.23.left_ref, ...), custom_call_target="tpu_custom_call" | custom-call | flops 2500000000 | bytes 2000000 | tf_op jit(solution)/shard_map/mix/pallas_call | solution.py:182
  72.2 0.4 collective-permute-start.5
  72.6 0.0 collective-permute-done.4.received_low
  72.6 1.2 %collective-permute-done.5.received_high = f32[2,4,64,128]{3,2,1,0:T(8,128)S(1)} collective-permute-done((f32[2,4,64,128]{3,2,1,0:T(8,128)S(1)}, f32[2,4,64,128]{3,2,1,0:T(8,128)S(1)}, u32[]{:S(2)}, u32[]{:S(2)}) %collective-permute-start.5) | collective-permute-done | bytes 262176 | tf_op jit(solution)/shard_map/ppermute | solution.py:337
  73.8 0.7 shard_map.55
  74.5 1.7 %collective-permute-start.6 = (f32[2,4,64,128]{3,2,1,0:T(8,128)S(1)}, f32[2,4,64,128]{3,2,1,0:T(8,128)S(1)}, u32[]{:S(2)}, u32[]{:S(2)}) collective-permute-start(f32[2,4,64,128]{3,2,1,0:T(8,128)S(1)} %get-tuple-element.34), channel_id=1, source_target_pairs={{0,1},{1,2},{2,3},{3,0},{4,12},{5,13},{6,14},{7,15},{8,9},{9,10},{... | collective-permute-start | bytes 786440 | tf_op jit(solution)/shard_map/ppermute | solution.py:347
  76.2 2.7 %collective-permute-start.7 = (f32[2,4,64,128]{3,2,1,0:T(8,128)S(1)}, f32[2,4,64,128]{3,2,1,0:T(8,128)S(1)}, u32[]{:S(2)}, u32[]{:S(2)}) collective-permute-start(f32[2,4,64,128]{3,2,1,0:T(8,128)S(1)} %get-tuple-element.35), channel_id=1, source_target_pairs={{0,2},{1,3},{2,0},{3,1},{4,20},{5,21},{6,22},{7,23},{8,10},{9,11},... | collective-permute-start | bytes 786440 | tf_op jit(solution)/shard_map/ppermute | solution.py:347
  78.9 1.4 %collective-permute-start.8 = (f32[2,4,64,128]{3,2,1,0:T(8,128)S(1)}, f32[2,4,64,128]{3,2,1,0:T(8,128)S(1)}, u32[]{:S(2)}, u32[]{:S(2)}) collective-permute-start(f32[2,4,64,128]{3,2,1,0:T(8,128)S(1)} %get-tuple-element.36), channel_id=1, source_target_pairs={{0,3},{1,0},{2,1},{3,2},{4,28},{5,29},{6,30},{7,31},{8,11},{9,8},{... | collective-permute-start | bytes 786440 | tf_op jit(solution)/shard_map/ppermute | solution.py:347
  80.3 5.5 %collective-permute-done.6.refs_1_ = f32[2,4,64,128]{3,2,1,0:T(8,128)S(1)} collective-permute-done((f32[2,4,64,128]{3,2,1,0:T(8,128)S(1)}, f32[2,4,64,128]{3,2,1,0:T(8,128)S(1)}, u32[]{:S(2)}, u32[]{:S(2)}) %collective-permute-start.6) | collective-permute-done | bytes 262176 | tf_op jit(solution)/shard_map/ppermute | solution.py:347
  85.8 3.2 %collective-permute-done.7.refs_2_ = f32[2,4,64,128]{3,2,1,0:T(8,128)S(1)} collective-permute-done((f32[2,4,64,128]{3,2,1,0:T(8,128)S(1)}, f32[2,4,64,128]{3,2,1,0:T(8,128)S(1)}, u32[]{:S(2)}, u32[]{:S(2)}) %collective-permute-start.7) | collective-permute-done | bytes 262176 | tf_op jit(solution)/shard_map/ppermute | solution.py:347
  89.1 0.0 collective-permute-done.8.refs_3_
  89.1 0.6 shard_map.56
  89.7 0.8 collective-permute-start.9
  90.5 2.8 %collective-permute-start.10 = (f32[4,2,64,128]{3,2,1,0:T(8,128)S(1)}, f32[4,2,64,128]{3,2,1,0:T(8,128)S(1)}, u32[]{:S(2)}, u32[]{:S(2)}) collective-permute-start(f32[4,2,64,128]{3,2,1,0:T(8,128)S(1)} %get-tuple-element.39), channel_id=1, source_target_pairs={{0,16},{1,17},{2,18},{3,19},{4,6},{5,7},{6,4},{7,5},{8,24},{9,25},... | collective-permute-start | bytes 786440 | tf_op jit(solution)/shard_map/ppermute | solution.py:352
  93.2 1.4 %collective-permute-start.11 = (f32[4,2,64,128]{3,2,1,0:T(8,128)S(1)}, f32[4,2,64,128]{3,2,1,0:T(8,128)S(1)}, u32[]{:S(2)}, u32[]{:S(2)}) collective-permute-start(f32[4,2,64,128]{3,2,1,0:T(8,128)S(1)} %get-tuple-element.40), channel_id=1, source_target_pairs={{0,24},{1,25},{2,26},{3,27},{4,7},{5,4},{6,5},{7,6},{8,0},{9,1},{1... | collective-permute-start | bytes 786440 | tf_op jit(solution)/shard_map/ppermute | solution.py:352
  94.6 0.0 all-to-all-done.1
  94.6 1.0 fill.1.held
  95.6 1.8 %collective-permute-done.9.rest_1_ = f32[4,2,64,128]{3,2,1,0:T(8,128)S(1)} collective-permute-done((f32[4,2,64,128]{3,2,1,0:T(8,128)S(1)}, f32[4,2,64,128]{3,2,1,0:T(8,128)S(1)}, u32[]{:S(2)}, u32[]{:S(2)}) %collective-permute-start.9) | collective-permute-done | bytes 262176 | tf_op jit(solution)/shard_map/ppermute | solution.py:352
  97.4 3.0 %collective-permute-done.10.rest_2_ = f32[4,2,64,128]{3,2,1,0:T(8,128)S(1)} collective-permute-done((f32[4,2,64,128]{3,2,1,0:T(8,128)S(1)}, f32[4,2,64,128]{3,2,1,0:T(8,128)S(1)}, u32[]{:S(2)}, u32[]{:S(2)}) %collective-permute-start.10) | collective-permute-done | bytes 262176 | tf_op jit(solution)/shard_map/ppermute | solution.py:352
  100.4 0.6 collective-permute-done.11.rest_3_
  101.0 1.6 %place.1 = f32[4,2,4,2,64,128]{5,4,3,2,1,0:T(8,128)} custom-call(s32[3]{0:T(128)S(1)} %pad_add_fusion.place, f32[4,2,4,2,64,128]{5,4,3,2,1,0:T(8,128)} %fill.1.held, f32[4,2,64,128]{3,2,1,0:T(8,128)S(1)} %get-tuple-element.37.rest_0_, f32[4,2,64,128]{3,2,1,0:T(8,128)S(1)} %collective-permute-done.9.rest_1_, ...), custom_call_target="tpu_custom_call", output_to_operand_aliasing={{}: (1, {})} | custom-call | flops 1000000 | bytes 4000000 | tf_op jit(solution)/shard_map/place/pallas_call | solution.py:277
  (1 shorter events, 0.0 us)
Async XLA Ops:
  0.0 48.0 %copy-start = (s32[64,2]{0,1:T(2,128)S(1)}, s32[64,2]{0,1:T(2,128)}, u32[]{:S(2)}) copy-start(s32[64,2]{0,1:T(2,128)} %param.7) | copy-start | bytes 1540
  35.7 14.5 %copy-start.2 = (f32[2,3,4]{2,0,1:T(2,128)S(1)}, f32[2,3,4]{2,0,1:T(2,128)}, u32[]{:S(2)}) copy-start(f32[2,3,4]{2,0,1:T(2,128)} %param.9) | copy-start | bytes 292
  35.8 23.1 %copy-start.1 = (s32[3]{0:T(128)S(1)}, s32[3]{0:T(128)}, u32[]{:S(2)}) copy-start(s32[3]{0:T(128)} %shifts.5) | copy-start | bytes 40
  35.8 17.3 %collective-permute-start = (f32[4,4,64,128]{3,2,1,0:T(8,128)S(1)}, f32[4,4,64,128]{3,2,1,0:T(8,128)S(1)}, u32[]{:S(2)}, u32[]{:S(2)}) collective-permute-start(f32[4,4,64,128]{3,2,1,0:T(8,128)S(1)} %get-tuple-element.25.rest_2_), channel_id=1, source_target_pairs={{0,32},{32,64},{64,96},{96,128},{128,160},{160,192},{192,224},{1,3... | collective-permute-start | bytes 1572872 | tf_op jit(solution)/shard_map/ppermute | solution.py:326
  40.9 18.0 %collective-permute-start.1 = (f32[4,4,64,128]{3,2,1,0:T(8,128)S(1)}, f32[4,4,64,128]{3,2,1,0:T(8,128)}, u32[]{:S(2)}, u32[]{:S(2)}) collective-permute-start(f32[4,4,64,128]{3,2,1,0:T(8,128)S(1)} %get-tuple-element.26.rest_1_), channel_id=1, source_target_pairs={{32,0},{64,32},{96,64},{128,96},{160,128},{192,160},{224,192},{33,... | collective-permute-start | bytes 1572872 | tf_op jit(solution)/shard_map/ppermute | solution.py:327
  42.9 24.2 %collective-permute-start.2 = (f32[4,4,64,128]{3,2,1,0:T(8,128)S(1)}, f32[4,4,64,128]{3,2,1,0:T(8,128)}, u32[]{:S(2)}, u32[]{:S(2)}) collective-permute-start(f32[4,4,64,128]{3,2,1,0:T(8,128)S(1)} %get-tuple-element.27.rest_2_.rest_1_), channel_id=1, source_target_pairs={{0,32},{32,64},{64,96},{96,128},{128,160},{160,192},{192,224},{1,3... | collective-permute-start | bytes 1572872 | tf_op jit(solution)/shard_map/ppermute | solution.py:326
  48.1 21.6 %collective-permute-start.3 = (f32[4,4,64,128]{3,2,1,0:T(8,128)S(1)}, f32[4,4,64,128]{3,2,1,0:T(8,128)}, u32[]{:S(2)}, u32[]{:S(2)}) collective-permute-start(f32[4,4,64,128]{3,2,1,0:T(8,128)S(1)} %get-tuple-element.28.rest_1_.rest_0_), channel_id=1, source_target_pairs={{32,0},{64,32},{96,64},{128,96},{160,128},{192,160},{224,192},{33,... | collective-permute-start | bytes 1572872 | tf_op jit(solution)/shard_map/ppermute | solution.py:327
  63.1 31.5 %all-to-all-start.1 = ((f32[32,64,128]{2,1,0:T(8,128)}), f32[32,64,128]{2,1,0:T(8,128)S(1)}, u32[]{:S(2)}, u32[]{:S(2)}) async-start(f32[32,64,128]{2,1,0:T(8,128)} %bitcast.5), calls=%async_computation.1 | async-start | bytes 2097152 | tf_op jit(solution)/shard_map/all_to_all | solution.py:349
  69.5 3.1 %collective-permute-start.4 = (f32[2,4,64,128]{3,2,1,0:T(8,128)S(1)}, f32[2,4,64,128]{3,2,1,0:T(8,128)S(1)}, u32[]{:S(2)}, u32[]{:S(2)}) collective-permute-start(f32[2,4,64,128]{3,2,1,0:T(8,128)S(1)} %get-tuple-element.31), channel_id=1, source_target_pairs={{0,4},{1,5},{2,6},{3,7},{4,0},{5,1},{6,2},{7,3},{8,12},{9,13},{10,... | collective-permute-start | bytes 786440 | tf_op jit(solution)/shard_map/ppermute | solution.py:337
  72.2 1.6 %collective-permute-start.5 = (f32[2,4,64,128]{3,2,1,0:T(8,128)S(1)}, f32[2,4,64,128]{3,2,1,0:T(8,128)S(1)}, u32[]{:S(2)}, u32[]{:S(2)}) collective-permute-start(f32[2,4,64,128]{3,2,1,0:T(8,128)S(1)} %get-tuple-element.32), channel_id=1, source_target_pairs={{0,4},{1,5},{2,6},{3,7},{4,0},{5,1},{6,2},{7,3},{8,12},{9,13},{10,... | collective-permute-start | bytes 786440 | tf_op jit(solution)/shard_map/ppermute | solution.py:337
  74.5 11.4 %collective-permute-start.6 = (f32[2,4,64,128]{3,2,1,0:T(8,128)S(1)}, f32[2,4,64,128]{3,2,1,0:T(8,128)S(1)}, u32[]{:S(2)}, u32[]{:S(2)}) collective-permute-start(f32[2,4,64,128]{3,2,1,0:T(8,128)S(1)} %get-tuple-element.34), channel_id=1, source_target_pairs={{0,1},{1,2},{2,3},{3,0},{4,12},{5,13},{6,14},{7,15},{8,9},{9,10},{... | collective-permute-start | bytes 786440 | tf_op jit(solution)/shard_map/ppermute | solution.py:347
  76.2 12.9 %collective-permute-start.7 = (f32[2,4,64,128]{3,2,1,0:T(8,128)S(1)}, f32[2,4,64,128]{3,2,1,0:T(8,128)S(1)}, u32[]{:S(2)}, u32[]{:S(2)}) collective-permute-start(f32[2,4,64,128]{3,2,1,0:T(8,128)S(1)} %get-tuple-element.35), channel_id=1, source_target_pairs={{0,2},{1,3},{2,0},{3,1},{4,20},{5,21},{6,22},{7,23},{8,10},{9,11},... | collective-permute-start | bytes 786440 | tf_op jit(solution)/shard_map/ppermute | solution.py:347
  78.9 10.2 %collective-permute-start.8 = (f32[2,4,64,128]{3,2,1,0:T(8,128)S(1)}, f32[2,4,64,128]{3,2,1,0:T(8,128)S(1)}, u32[]{:S(2)}, u32[]{:S(2)}) collective-permute-start(f32[2,4,64,128]{3,2,1,0:T(8,128)S(1)} %get-tuple-element.36), channel_id=1, source_target_pairs={{0,3},{1,0},{2,1},{3,2},{4,28},{5,29},{6,30},{7,31},{8,11},{9,8},{... | collective-permute-start | bytes 786440 | tf_op jit(solution)/shard_map/ppermute | solution.py:347
  89.7 7.7 %collective-permute-start.9 = (f32[4,2,64,128]{3,2,1,0:T(8,128)S(1)}, f32[4,2,64,128]{3,2,1,0:T(8,128)S(1)}, u32[]{:S(2)}, u32[]{:S(2)}) collective-permute-start(f32[4,2,64,128]{3,2,1,0:T(8,128)S(1)} %get-tuple-element.38), channel_id=1, source_target_pairs={{0,8},{1,9},{2,10},{3,11},{4,5},{5,6},{6,7},{7,4},{8,16},{9,17},{1... | collective-permute-start | bytes 786440 | tf_op jit(solution)/shard_map/ppermute | solution.py:352
  90.5 9.9 %collective-permute-start.10 = (f32[4,2,64,128]{3,2,1,0:T(8,128)S(1)}, f32[4,2,64,128]{3,2,1,0:T(8,128)S(1)}, u32[]{:S(2)}, u32[]{:S(2)}) collective-permute-start(f32[4,2,64,128]{3,2,1,0:T(8,128)S(1)} %get-tuple-element.39), channel_id=1, source_target_pairs={{0,16},{1,17},{2,18},{3,19},{4,6},{5,7},{6,4},{7,5},{8,24},{9,25},... | collective-permute-start | bytes 786440 | tf_op jit(solution)/shard_map/ppermute | solution.py:352
  93.2 7.8 %collective-permute-start.11 = (f32[4,2,64,128]{3,2,1,0:T(8,128)S(1)}, f32[4,2,64,128]{3,2,1,0:T(8,128)S(1)}, u32[]{:S(2)}, u32[]{:S(2)}) collective-permute-start(f32[4,2,64,128]{3,2,1,0:T(8,128)S(1)} %get-tuple-element.40), channel_id=1, source_target_pairs={{0,24},{1,25},{2,26},{3,27},{4,7},{5,4},{6,5},{7,6},{8,0},{9,1},{1... | collective-permute-start | bytes 786440 | tf_op jit(solution)/shard_map/ppermute | solution.py:352
where the time goes:
time: 103 us
  blocking collectives  35.7 us (35%)
  starting transfers between devices  29.4 us (29%)
  waiting for transfers between devices  22.4 us (22%)
  Pallas kernels  14.8 us (14%)
    all_to_all x1, blocking collectives, on_device(): lax.all_to_all(green_less.reshape(group, owned, rows, columns), GROUP, 0,...  35.7 us
    ppermute x2, starting transfers between devices, on_device(): below = lax.ppermute(high, 'z', up)  10.2 us
    pallas_call x3, Pallas kernels, mix(): pl.pallas_call(functools.partial(mix_kernel, split, pair), in_specs=[smem...  9.03 us
    ppermute x3, waiting for transfers between devices, on_device(): arrived[step] = lax.ppermute(arrived[step], AXES, along(step, 0))  8.74 us
    ppermute x3, starting transfers between devices, on_device(): arrived[step] = lax.ppermute(arrived[step], AXES, along(step, 0))  5.85 us
    ppermute x2, waiting for transfers between devices, on_device(): above = lax.ppermute(low, 'z', down)  5.72 us
    ppermute x3, waiting for transfers between devices, on_device(): landed[step] = lax.ppermute(landed[step], AXES, along(step, 1))  5.45 us
    ppermute x3, starting transfers between devices, on_device(): landed[step] = lax.ppermute(landed[step], AXES, along(step, 1))  4.88 us
  transfers between devices with their start and end apart: 13, of which 8 were waited for; matrix products, arithmetic and copies ran while one was open for 0% of the time, Pallas kernels for 13%

commit v1 on v0

--- a/solution.py
+++ b/solution.py
@@ -194,18 +194,18 @@
 def sort_kernel(place, kept_low, kept_high, received_low, received_high, *targets):
     core, first = place[0], place[1]
     half = kept_low.shape[0]
-    whole = targets[-1]
-    targets = targets[:-1]
-    for side, pieces in enumerate(((kept_low, kept_high), (received_low, received_high))):
-        for x in range(2 * half):
-            whole[side, x] = pieces[x // half][x % half]
+
+    def pick(low, high, x, moment):
+        row = lax.rem(x, half)
+        return jnp.where(x < half, low[row, moment], high[row, moment])
+
     for step, target in enumerate(targets):
         where = lax.rem(first + step, 4)
         for other in range(4):
             x = jnp.where(core == 0, other, where)
             moment = jnp.where(core == 0, where, other)
-            target[core, other] = whole[0, x, moment]
-            target[1 - core, other] = whole[1, x, moment]
+            target[core, other] = pick(kept_low, kept_high, x, moment)
+            target[1 - core, other] = pick(received_low, received_high, x, moment)
 
 
 def turn_kernel(place, *refs):
@@ -336,13 +336,7 @@
         stay, away = compute(True, 0, upper, 3)
         received.append(lax.ppermute(away, AXES, ring(lambda x, c, y: (x, 1 - c, y))))
         kept.append(stay)
-    arrived = move(
-        sort_kernel,
-        place,
-        (*kept, *received),
-        (2, 4, rows, columns),
-        [pltpu.VMEM((2, 4, 4, rows, columns), jnp.float32)],
-    )
+    arrived = move(sort_kernel, place, (*kept, *received), (2, 4, rows, columns))
     for step in (2, 1, 3):
         arrived[step] = lax.ppermute(arrived[step], AXES, along(step, 0))
     (result,) = compute(False, 1, 0, 4)

time: 103 us -> 103 us (level)
  no operation moved by 1% of the time
where the time goes in v1:
time: 103 us
  blocking collectives  35.7 us (35%)
  starting transfers between devices  29.4 us (29%)
  waiting for transfers between devices  22.3 us (22%)
  Pallas kernels  14.9 us (14%)
    all_to_all x1, blocking collectives, on_device(): lax.all_to_all(green_less.reshape(group, owned, rows, columns), GROUP, 0,...  35.7 us
    ppermute x2, starting transfers between devices, on_device(): below = lax.ppermute(high, 'z', up)  10.2 us
    pallas_call x3, Pallas kernels, mix(): pl.pallas_call(functools.partial(mix_kernel, split, pair), in_specs=[smem...  9.03 us
    ppermute x3, waiting for transfers between devices, on_device(): arrived[step] = lax.ppermute(arrived[step], AXES, along(step, 0))  8.66 us
    ppermute x3, starting transfers between devices, on_device(): arrived[step] = lax.ppermute(arrived[step], AXES, along(step, 0))  5.85 us
    ppermute x2, waiting for transfers between devices, on_device(): above = lax.ppermute(low, 'z', down)  5.72 us
    ppermute x3, waiting for transfers between devices, on_device(): landed[step] = lax.ppermute(landed[step], AXES, along(step, 1))  5.45 us
    ppermute x3, starting transfers between devices, on_device(): landed[step] = lax.ppermute(landed[step], AXES, along(step, 1))  4.88 us
  transfers between devices with their start and end apart: 13, of which 8 were waited for; matrix products, arithmetic and copies ran while one was open for 0% of the time, Pallas kernels for 13%

profile of v1, /device:TPU:96, one launch (start us, length us, event | category | flops | bytes accessed | tf_op | source)
XLA Modules:
  0.0 102.7 jit_solution(2204133996877796004)
XLA Ops:
  0.0 0.0 copy-start
  0.0 35.7 %all_to_all.10 = f32[32,2,64,128]{3,2,1,0:T(8,128)S(1)} all-to-all(f32[32,2,64,128]{3,2,1,0:T(8,128)} %bitcast.11), channel_id=1, replica_groups=mesh['z'=8,'x'=4,'c'=2,'y'=4] {'x','c','y'}, dimensions={0} | all-to-all | bytes 4194304 | tf_op jit(solution)/shard_map/all_to_all | solution.py:319
  35.7 0.0 copy-start.2
  35.7 0.1 fold.2
  35.8 0.0 copy-start.1
  35.8 5.0 %collective-permute-start = (f32[4,4,64,128]{3,2,1,0:T(8,128)S(1)}, f32[4,4,64,128]{3,2,1,0:T(8,128)S(1)}, u32[]{:S(2)}, u32[]{:S(2)}) collective-permute-start(f32[4,4,64,128]{3,2,1,0:T(8,128)S(1)} %get-tuple-element.25.rest_2_), channel_id=1, source_target_pairs={{0,32},{32,64},{64,96},{96,128},{128,160},{160,192},{192,224},{1,3... | collective-permute-start | bytes 1572872 | tf_op jit(solution)/shard_map/ppermute | solution.py:326
  40.9 1.9 %collective-permute-start.1 = (f32[4,4,64,128]{3,2,1,0:T(8,128)S(1)}, f32[4,4,64,128]{3,2,1,0:T(8,128)}, u32[]{:S(2)}, u32[]{:S(2)}) collective-permute-start(f32[4,4,64,128]{3,2,1,0:T(8,128)S(1)} %get-tuple-element.26.rest_1_), channel_id=1, source_target_pairs={{32,0},{64,32},{96,64},{128,96},{160,128},{192,160},{224,192},{33,... | collective-permute-start | bytes 1572872 | tf_op jit(solution)/shard_map/ppermute | solution.py:327
  42.8 0.1 fold.3
  42.9 5.1 %collective-permute-start.2 = (f32[4,4,64,128]{3,2,1,0:T(8,128)S(1)}, f32[4,4,64,128]{3,2,1,0:T(8,128)}, u32[]{:S(2)}, u32[]{:S(2)}) collective-permute-start(f32[4,4,64,128]{3,2,1,0:T(8,128)S(1)} %get-tuple-element.27.rest_2_.rest_1_), channel_id=1, source_target_pairs={{0,32},{32,64},{64,96},{96,128},{128,160},{160,192},{192,224},{1,3... | collective-permute-start | bytes 1572872 | tf_op jit(solution)/shard_map/ppermute | solution.py:326
  48.0 0.0 copy-done
  48.1 0.1 constant_dynamic-slice_fusion
  48.1 1.9 %collective-permute-start.3 = (f32[4,4,64,128]{3,2,1,0:T(8,128)S(1)}, f32[4,4,64,128]{3,2,1,0:T(8,128)}, u32[]{:S(2)}, u32[]{:S(2)}) collective-permute-start(f32[4,4,64,128]{3,2,1,0:T(8,128)S(1)} %get-tuple-element.28.rest_1_.rest_0_), channel_id=1, source_target_pairs={{32,0},{64,32},{96,64},{128,96},{160,128},{192,160},{224,192},{33,... | collective-permute-start | bytes 1572872 | tf_op jit(solution)/shard_map/ppermute | solution.py:327
  50.0 0.1 pad_add_fusion.place
  50.1 0.1 copy.11.atoms
  50.2 0.0 copy-done.2
  50.2 1.7 %tables.1 = (bf16[2,64,384]{2,1,0:T(8,128)(2,1)S(1)}, bf16[2,3,2,128,128]{4,3,2,1,0:T(8,128)(2,1)S(1)}) custom-call(s32[2,2]{1,0:T(2,128)S(1)} %copy.11.atoms, bf16[32,3,64,64]{3,2,1,0:T(8,128)(2,1)} %coupling_hbm.1), custom_call_target="tpu_custom_call" | custom-call | flops 1000000 | bytes 4000000 | tf_op jit(solution)/shard_map/tables/pallas_call | solution.py:49
  51.9 1.2 %collective-permute-done.rest_0_ = f32[4,4,64,128]{3,2,1,0:T(8,128)S(1)} collective-permute-done((f32[4,4,64,128]{3,2,1,0:T(8,128)S(1)}, f32[4,4,64,128]{3,2,1,0:T(8,128)S(1)}, u32[]{:S(2)}, u32[]{:S(2)}) %collective-permute-start) | collective-permute-done | bytes 524320 | tf_op jit(solution)/shard_map/ppermute | solution.py:326
  53.2 5.7 %collective-permute-done.1.rest_3_ = f32[4,4,64,128]{3,2,1,0:T(8,128)} collective-permute-done((f32[4,4,64,128]{3,2,1,0:T(8,128)S(1)}, f32[4,4,64,128]{3,2,1,0:T(8,128)}, u32[]{:S(2)}, u32[]{:S(2)}) %collective-permute-start.1) | collective-permute-done | bytes 524320 | tf_op jit(solution)/shard_map/ppermute | solution.py:327
  58.9 0.0 copy-done.1
  58.9 4.2 %mix.3 = f32[8,4,64,128]{3,2,1,0:T(8,128)} custom-call(s32[3]{0:T(128)S(1)} %pad_add_fusion.place, s32[3]{0:T(128)S(1)} %copy-done.1, f32[2,3,4]{2,1,0:T(4,128)S(1)} %copy.8.weights, bf16[2,64,384]{2,1,0:T(8,128)(2,1)S(1)} %get-tuple-element.23.left_ref, bf16[2,3,2,128,128]{4,3,2,1,0:T(8,128)(2,1)S(1)} %get-tuple-element.24.right_ref, ...), custom_call_target="tpu_custom_call" | custom-call | flops 2500000000 | bytes 2000000 | tf_op jit(solution)/shard_map/mix/pallas_call | solution.py:182
  63.1 3.9 %all-to-all-start.1 = ((f32[32,64,128]{2,1,0:T(8,128)}), f32[32,64,128]{2,1,0:T(8,128)S(1)}, u32[]{:S(2)}, u32[]{:S(2)}) async-start(f32[32,64,128]{2,1,0:T(8,128)} %bitcast.5), calls=%async_computation.1 | async-start | bytes 2097152 | tf_op jit(solution)/shard_map/all_to_all | solution.py:343
  67.0 0.0 collective-permute-done.2.rest_0_
  67.1 2.4 %mix.4 = (f32[2,4,64,128]{3,2,1,0:T(8,128)S(1)}, f32[2,4,64,128]{3,2,1,0:T(8,128)S(1)}) custom-call(s32[3]{0:T(128)S(1)} %pad_add_fusion.place, s32[3]{0:T(128)S(1)} %copy-done.1, f32[2,3,4]{2,1,0:T(4,128)S(1)} %copy.8.weights, bf16[2,64,384]{2,1,0:T(8,128)(2,1)S(1)} %get-tuple-element.23.left_ref, ...), custom_call_target="tpu_custom_call" | custom-call | flops 2500000000 | bytes 2000000 | tf_op jit(solution)/shard_map/mix/pallas_call | solution.py:182
  69.5 0.3 collective-permute-start.4
  69.8 0.0 collective-permute-done.3.rest_2_
  69.8 2.4 %mix.5 = (f32[2,4,64,128]{3,2,1,0:T(8,128)S(1)}, f32[2,4,64,128]{3,2,1,0:T(8,128)S(1)}) custom-call(s32[3]{0:T(128)S(1)} %pad_add_fusion.place, s32[3]{0:T(128)S(1)} %copy-done.1, f32[2,3,4]{2,1,0:T(4,128)S(1)} %copy.8.weights, bf16[2,64,384]{2,1,0:T(8,128)(2,1)S(1)} %get-tuple-element.23.left_ref, ...), custom_call_target="tpu_custom_call" | custom-call | flops 2500000000 | bytes 2000000 | tf_op jit(solution)/shard_map/mix/pallas_call | solution.py:182
  72.2 0.4 collective-permute-start.5
  72.6 0.0 collective-permute-done.4.received_low
  72.6 1.2 %collective-permute-done.5.received_high = f32[2,4,64,128]{3,2,1,0:T(8,128)S(1)} collective-permute-done((f32[2,4,64,128]{3,2,1,0:T(8,128)S(1)}, f32[2,4,64,128]{3,2,1,0:T(8,128)S(1)}, u32[]{:S(2)}, u32[]{:S(2)}) %collective-permute-start.5) | collective-permute-done | bytes 262176 | tf_op jit(solution)/shard_map/ppermute | solution.py:337
  73.8 0.8 shard_map.55
  74.6 1.7 %collective-permute-start.6 = (f32[2,4,64,128]{3,2,1,0:T(8,128)S(1)}, f32[2,4,64,128]{3,2,1,0:T(8,128)S(1)}, u32[]{:S(2)}, u32[]{:S(2)}) collective-permute-start(f32[2,4,64,128]{3,2,1,0:T(8,128)S(1)} %get-tuple-element.34), channel_id=1, source_target_pairs={{0,1},{1,2},{2,3},{3,0},{4,12},{5,13},{6,14},{7,15},{8,9},{9,10},{... | collective-permute-start | bytes 786440 | tf_op jit(solution)/shard_map/ppermute | solution.py:341
  76.3 2.7 %collective-permute-start.7 = (f32[2,4,64,128]{3,2,1,0:T(8,128)S(1)}, f32[2,4,64,128]{3,2,1,0:T(8,128)S(1)}, u32[]{:S(2)}, u32[]{:S(2)}) collective-permute-start(f32[2,4,64,128]{3,2,1,0:T(8,128)S(1)} %get-tuple-element.35), channel_id=1, source_target_pairs={{0,2},{1,3},{2,0},{3,1},{4,20},{5,21},{6,22},{7,23},{8,10},{9,11},... | collective-permute-start | bytes 786440 | tf_op jit(solution)/shard_map/ppermute | solution.py:341
  79.0 1.4 %collective-permute-start.8 = (f32[2,4,64,128]{3,2,1,0:T(8,128)S(1)}, f32[2,4,64,128]{3,2,1,0:T(8,128)S(1)}, u32[]{:S(2)}, u32[]{:S(2)}) collective-permute-start(f32[2,4,64,128]{3,2,1,0:T(8,128)S(1)} %get-tuple-element.36), channel_id=1, source_target_pairs={{0,3},{1,0},{2,1},{3,2},{4,28},{5,29},{6,30},{7,31},{8,11},{9,8},{... | collective-permute-start | bytes 786440 | tf_op jit(solution)/shard_map/ppermute | solution.py:341
  80.4 5.4 %collective-permute-done.6.refs_1_ = f32[2,4,64,128]{3,2,1,0:T(8,128)S(1)} collective-permute-done((f32[2,4,64,128]{3,2,1,0:T(8,128)S(1)}, f32[2,4,64,128]{3,2,1,0:T(8,128)S(1)}, u32[]{:S(2)}, u32[]{:S(2)}) %collective-permute-start.6) | collective-permute-done | bytes 262176 | tf_op jit(solution)/shard_map/ppermute | solution.py:341
  85.9 3.2 %collective-permute-done.7.refs_2_ = f32[2,4,64,128]{3,2,1,0:T(8,128)S(1)} collective-permute-done((f32[2,4,64,128]{3,2,1,0:T(8,128)S(1)}, f32[2,4,64,128]{3,2,1,0:T(8,128)S(1)}, u32[]{:S(2)}, u32[]{:S(2)}) %collective-permute-start.7) | collective-permute-done | bytes 262176 | tf_op jit(solution)/shard_map/ppermute | solution.py:341
  89.1 0.0 collective-permute-done.8.refs_3_
  89.1 0.6 shard_map.56
  89.7 0.8 collective-permute-start.9
  90.5 2.8 %collective-permute-start.10 = (f32[4,2,64,128]{3,2,1,0:T(8,128)S(1)}, f32[4,2,64,128]{3,2,1,0:T(8,128)S(1)}, u32[]{:S(2)}, u32[]{:S(2)}) collective-permute-start(f32[4,2,64,128]{3,2,1,0:T(8,128)S(1)} %get-tuple-element.39), channel_id=1, source_target_pairs={{0,16},{1,17},{2,18},{3,19},{4,6},{5,7},{6,4},{7,5},{8,24},{9,25},... | collective-permute-start | bytes 786440 | tf_op jit(solution)/shard_map/ppermute | solution.py:346
  93.2 1.4 %collective-permute-start.11 = (f32[4,2,64,128]{3,2,1,0:T(8,128)S(1)}, f32[4,2,64,128]{3,2,1,0:T(8,128)S(1)}, u32[]{:S(2)}, u32[]{:S(2)}) collective-permute-start(f32[4,2,64,128]{3,2,1,0:T(8,128)S(1)} %get-tuple-element.40), channel_id=1, source_target_pairs={{0,24},{1,25},{2,26},{3,27},{4,7},{5,4},{6,5},{7,6},{8,0},{9,1},{1... | collective-permute-start | bytes 786440 | tf_op jit(solution)/shard_map/ppermute | solution.py:346
  94.6 0.0 all-to-all-done.1
  94.6 1.0 fill.1.held
  95.6 1.8 %collective-permute-done.9.rest_1_ = f32[4,2,64,128]{3,2,1,0:T(8,128)S(1)} collective-permute-done((f32[4,2,64,128]{3,2,1,0:T(8,128)S(1)}, f32[4,2,64,128]{3,2,1,0:T(8,128)S(1)}, u32[]{:S(2)}, u32[]{:S(2)}) %collective-permute-start.9) | collective-permute-done | bytes 262176 | tf_op jit(solution)/shard_map/ppermute | solution.py:346
  97.4 3.0 %collective-permute-done.10.rest_2_ = f32[4,2,64,128]{3,2,1,0:T(8,128)S(1)} collective-permute-done((f32[4,2,64,128]{3,2,1,0:T(8,128)S(1)}, f32[4,2,64,128]{3,2,1,0:T(8,128)S(1)}, u32[]{:S(2)}, u32[]{:S(2)}) %collective-permute-start.10) | collective-permute-done | bytes 262176 | tf_op jit(solution)/shard_map/ppermute | solution.py:346
  100.4 0.6 collective-permute-done.11.rest_3_
  101.0 1.6 %place.1 = f32[4,2,4,2,64,128]{5,4,3,2,1,0:T(8,128)} custom-call(s32[3]{0:T(128)S(1)} %pad_add_fusion.place, f32[4,2,4,2,64,128]{5,4,3,2,1,0:T(8,128)} %fill.1.held, f32[4,2,64,128]{3,2,1,0:T(8,128)S(1)} %get-tuple-element.37.rest_0_, f32[4,2,64,128]{3,2,1,0:T(8,128)S(1)} %collective-permute-done.9.rest_1_, ...), custom_call_target="tpu_custom_call", output_to_operand_aliasing={{}: (1, {})} | custom-call | flops 1000000 | bytes 4000000 | tf_op jit(solution)/shard_map/place/pallas_call | solution.py:277
  (1 shorter events, 0.0 us)
Async XLA Ops:
  0.0 48.0 %copy-start = (s32[64,2]{0,1:T(2,128)S(1)}, s32[64,2]{0,1:T(2,128)}, u32[]{:S(2)}) copy-start(s32[64,2]{0,1:T(2,128)} %param.7) | copy-start | bytes 1540
  35.7 14.5 %copy-start.2 = (f32[2,3,4]{2,0,1:T(2,128)S(1)}, f32[2,3,4]{2,0,1:T(2,128)}, u32[]{:S(2)}) copy-start(f32[2,3,4]{2,0,1:T(2,128)} %param.9) | copy-start | bytes 292
  35.8 23.1 %copy-start.1 = (s32[3]{0:T(128)S(1)}, s32[3]{0:T(128)}, u32[]{:S(2)}) copy-start(s32[3]{0:T(128)} %shifts.5) | copy-start | bytes 40
  35.8 17.3 %collective-permute-start = (f32[4,4,64,128]{3,2,1,0:T(8,128)S(1)}, f32[4,4,64,128]{3,2,1,0:T(8,128)S(1)}, u32[]{:S(2)}, u32[]{:S(2)}) collective-permute-start(f32[4,4,64,128]{3,2,1,0:T(8,128)S(1)} %get-tuple-element.25.rest_2_), channel_id=1, source_target_pairs={{0,32},{32,64},{64,96},{96,128},{128,160},{160,192},{192,224},{1,3... | collective-permute-start | bytes 1572872 | tf_op jit(solution)/shard_map/ppermute | solution.py:326
  40.9 18.0 %collective-permute-start.1 = (f32[4,4,64,128]{3,2,1,0:T(8,128)S(1)}, f32[4,4,64,128]{3,2,1,0:T(8,128)}, u32[]{:S(2)}, u32[]{:S(2)}) collective-permute-start(f32[4,4,64,128]{3,2,1,0:T(8,128)S(1)} %get-tuple-element.26.rest_1_), channel_id=1, source_target_pairs={{32,0},{64,32},{96,64},{128,96},{160,128},{192,160},{224,192},{33,... | collective-permute-start | bytes 1572872 | tf_op jit(solution)/shard_map/ppermute | solution.py:327
  42.9 24.2 %collective-permute-start.2 = (f32[4,4,64,128]{3,2,1,0:T(8,128)S(1)}, f32[4,4,64,128]{3,2,1,0:T(8,128)}, u32[]{:S(2)}, u32[]{:S(2)}) collective-permute-start(f32[4,4,64,128]{3,2,1,0:T(8,128)S(1)} %get-tuple-element.27.rest_2_.rest_1_), channel_id=1, source_target_pairs={{0,32},{32,64},{64,96},{96,128},{128,160},{160,192},{192,224},{1,3... | collective-permute-start | bytes 1572872 | tf_op jit(solution)/shard_map/ppermute | solution.py:326
  48.1 21.6 %collective-permute-start.3 = (f32[4,4,64,128]{3,2,1,0:T(8,128)S(1)}, f32[4,4,64,128]{3,2,1,0:T(8,128)}, u32[]{:S(2)}, u32[]{:S(2)}) collective-permute-start(f32[4,4,64,128]{3,2,1,0:T(8,128)S(1)} %get-tuple-element.28.rest_1_.rest_0_), channel_id=1, source_target_pairs={{32,0},{64,32},{96,64},{128,96},{160,128},{192,160},{224,192},{33,... | collective-permute-start | bytes 1572872 | tf_op jit(solution)/shard_map/ppermute | solution.py:327
  63.1 31.5 %all-to-all-start.1 = ((f32[32,64,128]{2,1,0:T(8,128)}), f32[32,64,128]{2,1,0:T(8,128)S(1)}, u32[]{:S(2)}, u32[]{:S(2)}) async-start(f32[32,64,128]{2,1,0:T(8,128)} %bitcast.5), calls=%async_computation.1 | async-start | bytes 2097152 | tf_op jit(solution)/shard_map/all_to_all | solution.py:343
  69.5 3.1 %collective-permute-start.4 = (f32[2,4,64,128]{3,2,1,0:T(8,128)S(1)}, f32[2,4,64,128]{3,2,1,0:T(8,128)S(1)}, u32[]{:S(2)}, u32[]{:S(2)}) collective-permute-start(f32[2,4,64,128]{3,2,1,0:T(8,128)S(1)} %get-tuple-element.31), channel_id=1, source_target_pairs={{0,4},{1,5},{2,6},{3,7},{4,0},{5,1},{6,2},{7,3},{8,12},{9,13},{10,... | collective-permute-start | bytes 786440 | tf_op jit(solution)/shard_map/ppermute | solution.py:337
  72.2 1.6 %collective-permute-start.5 = (f32[2,4,64,128]{3,2,1,0:T(8,128)S(1)}, f32[2,4,64,128]{3,2,1,0:T(8,128)S(1)}, u32[]{:S(2)}, u32[]{:S(2)}) collective-permute-start(f32[2,4,64,128]{3,2,1,0:T(8,128)S(1)} %get-tuple-element.32), channel_id=1, source_target_pairs={{0,4},{1,5},{2,6},{3,7},{4,0},{5,1},{6,2},{7,3},{8,12},{9,13},{10,... | collective-permute-start | bytes 786440 | tf_op jit(solution)/shard_map/ppermute | solution.py:337
  74.6 11.3 %collective-permute-start.6 = (f32[2,4,64,128]{3,2,1,0:T(8,128)S(1)}, f32[2,4,64,128]{3,2,1,0:T(8,128)S(1)}, u32[]{:S(2)}, u32[]{:S(2)}) collective-permute-start(f32[2,4,64,128]{3,2,1,0:T(8,128)S(1)} %get-tuple-element.34), channel_id=1, source_target_pairs={{0,1},{1,2},{2,3},{3,0},{4,12},{5,13},{6,14},{7,15},{8,9},{9,10},{... | collective-permute-start | bytes 786440 | tf_op jit(solution)/shard_map/ppermute | solution.py:341
  76.3 12.8 %collective-permute-start.7 = (f32[2,4,64,128]{3,2,1,0:T(8,128)S(1)}, f32[2,4,64,128]{3,2,1,0:T(8,128)S(1)}, u32[]{:S(2)}, u32[]{:S(2)}) collective-permute-start(f32[2,4,64,128]{3,2,1,0:T(8,128)S(1)} %get-tuple-element.35), channel_id=1, source_target_pairs={{0,2},{1,3},{2,0},{3,1},{4,20},{5,21},{6,22},{7,23},{8,10},{9,11},... | collective-permute-start | bytes 786440 | tf_op jit(solution)/shard_map/ppermute | solution.py:341
  79.0 10.1 %collective-permute-start.8 = (f32[2,4,64,128]{3,2,1,0:T(8,128)S(1)}, f32[2,4,64,128]{3,2,1,0:T(8,128)S(1)}, u32[]{:S(2)}, u32[]{:S(2)}) collective-permute-start(f32[2,4,64,128]{3,2,1,0:T(8,128)S(1)} %get-tuple-element.36), channel_id=1, source_target_pairs={{0,3},{1,0},{2,1},{3,2},{4,28},{5,29},{6,30},{7,31},{8,11},{9,8},{... | collective-permute-start | bytes 786440 | tf_op jit(solution)/shard_map/ppermute | solution.py:341
  89.7 7.7 %collective-permute-start.9 = (f32[4,2,64,128]{3,2,1,0:T(8,128)S(1)}, f32[4,2,64,128]{3,2,1,0:T(8,128)S(1)}, u32[]{:S(2)}, u32[]{:S(2)}) collective-permute-start(f32[4,2,64,128]{3,2,1,0:T(8,128)S(1)} %get-tuple-element.38), channel_id=1, source_target_pairs={{0,8},{1,9},{2,10},{3,11},{4,5},{5,6},{6,7},{7,4},{8,16},{9,17},{1... | collective-permute-start | bytes 786440 | tf_op jit(solution)/shard_map/ppermute | solution.py:346
  90.5 9.9 %collective-permute-start.10 = (f32[4,2,64,128]{3,2,1,0:T(8,128)S(1)}, f32[4,2,64,128]{3,2,1,0:T(8,128)S(1)}, u32[]{:S(2)}, u32[]{:S(2)}) collective-permute-start(f32[4,2,64,128]{3,2,1,0:T(8,128)S(1)} %get-tuple-element.39), channel_id=1, source_target_pairs={{0,16},{1,17},{2,18},{3,19},{4,6},{5,7},{6,4},{7,5},{8,24},{9,25},... | collective-permute-start | bytes 786440 | tf_op jit(solution)/shard_map/ppermute | solution.py:346
  93.2 7.8 %collective-permute-start.11 = (f32[4,2,64,128]{3,2,1,0:T(8,128)S(1)}, f32[4,2,64,128]{3,2,1,0:T(8,128)S(1)}, u32[]{:S(2)}, u32[]{:S(2)}) collective-permute-start(f32[4,2,64,128]{3,2,1,0:T(8,128)S(1)} %get-tuple-element.40), channel_id=1, source_target_pairs={{0,24},{1,25},{2,26},{3,27},{4,7},{5,4},{6,5},{7,6},{8,0},{9,1},{1... | collective-permute-start | bytes 786440 | tf_op jit(solution)/shard_map/ppermute | solution.py:346
